TPU v7x, 32 devices: a whole 2x2x4 slice. The times are simulated.
32 devices in a mesh: dom: 8 (over z, x), group: 4 (over y, core).
Axes of the slice: x: 2, y: 2, z: 4, core: 2. Of those that a mesh axis runs over, the one named last changes fastest.
Arguments:
- features: bfloat16 [65536, 256], P(('dom', 'group')), may hold values from -6 to 6
- boundary: int32 [2048], P(('dom', 'group')), may hold values from 0 to 127, as said below
- request: int32 [128, 24], P(('dom', 'group')), may hold values from 0 to 63, as said below
- tile_slots: int32 [512, 8], P(('dom', 'group')), may hold values from 0 to 223, as said below
- neighbors: int32 [65536, 10], P(('dom', 'group')), may hold values from 0 to 127
- negatives: int32 [65536, 4], P(('dom', 'group')), may hold values from 0 to 127
- layer_weight: bfloat16 [512, 256], replicated, may hold values from -0.25 to 0.25
Outputs:
- feature_grad: float32 [65536, 256], P(('dom', 'group'))
- weight_grad: float32 [512, 256], replicated
- loss_mean: float32 [], replicated
Inputs may be any that keep to these rules, and one draw needn't show every extreme that they name: The 64 entries boundary[i * 64 to i * 64 + 63] are distinct numbers of device i's own row blocks. `request`: row i * 4 + e holds 24 distinct positions in the boundary list of device (i // 4) * 4 + e. `tile_slots`: entries are numbers s as in the first step; the 128 entries of one device are distinct and include every number from 128 to 223.
All inputs are finite; a program needn't handle non-finite values.
Results may differ from a plain program's by a relative error of at most 0.00075.
The roundings to bfloat16 on the way count: a program that leaves them out, or rounds other values in their place, can miss the bound.
Values may be sent and summed in bfloat16 or wider, within the bound.
No kernel may reach another device: no remote copies, remote signals or barrier semaphores. Data moves between devices by JAX's collectives and lax.ppermute only.
A program may use at most 64 MiB of HBM per device.

v0:
```python
import jax
import jax.numpy as jnp
from jax import lax
from jax.sharding import PartitionSpec as P

TILE = 128
BLK = 16
NBT = 8
DEG = 10
NNEG = 4
margin = 0.5
epsilon = 1e-06


def contract(form, left, right):
    return jnp.einsum(form, left, right, preferred_element_type=jnp.float32)


def tile_terms(own_rows, candidates, neighbor_ids, negative_ids, layer_weight):
    tile_count, tile_rows, feature_width = own_rows.shape
    cand_count = candidates.shape[1]
    degree = neighbor_ids.shape[-1]
    negative_count = negative_ids.shape[-1]
    slot_ids = jnp.arange(cand_count, dtype=jnp.int32)
    counts = jnp.sum((neighbor_ids[..., None] == slot_ids).astype(jnp.float32), axis=2).astype(
        jnp.bfloat16
    )
    aggregate = (contract("tuc,tcd->tud", counts, candidates) / degree).astype(jnp.bfloat16)
    joined = jnp.concatenate([own_rows, aggregate], axis=-1).reshape(-1, 2 * feature_width)
    preact = jnp.dot(joined, layer_weight, preferred_element_type=jnp.float32)
    gate_value = jax.nn.sigmoid(preact)
    hidden = preact * gate_value
    norm_scale = lax.rsqrt(jnp.mean(hidden * hidden, axis=-1, keepdims=True) + epsilon)
    embedding = hidden * norm_scale
    embed_half = embedding.astype(jnp.bfloat16).reshape(tile_count, tile_rows, feature_width)
    inv_root = feature_width ** (-0.5)
    scores = contract("tud,tcd->tuc", embed_half, candidates) * inv_root
    positive = (neighbor_ids[..., 0:1] == slot_ids).astype(jnp.float32)
    negative = (negative_ids[..., None] == slot_ids).astype(jnp.float32)
    pos_score = jnp.sum(scores * positive, axis=-1, keepdims=True)
    neg_score = jnp.sum(scores[:, :, None, :] * negative, axis=-1)
    excess = margin + neg_score - pos_score
    loss_sum = jnp.sum(jax.nn.softplus(excess)) / negative_count
    neg_weight = jax.nn.sigmoid(excess) / negative_count
    dscores = (
        jnp.sum(neg_weight[..., None] * negative, axis=2)
        - jnp.sum(neg_weight, axis=-1, keepdims=True) * positive
    ) * inv_root
    dscores_half = dscores.astype(jnp.bfloat16)
    dembedding = contract("tuc,tcd->tud", dscores_half, candidates).reshape(-1, feature_width)
    dcandidates = contract("tuc,tud->tcd", dscores_half, embed_half)
    dhidden = norm_scale * (
        dembedding - embedding * jnp.mean(dembedding * embedding, axis=-1, keepdims=True)
    )
    dpreact = (dhidden * gate_value * (1.0 + preact * (1.0 - gate_value))).astype(jnp.bfloat16)
    dweight = jnp.dot(joined.T, dpreact, preferred_element_type=jnp.float32)
    dinputs = jnp.dot(dpreact, layer_weight.T, preferred_element_type=jnp.float32)
    dself = dinputs[:, :feature_width].reshape(tile_count, tile_rows, feature_width)
    daggregate = (
        (dinputs[:, feature_width:] / degree)
        .astype(jnp.bfloat16)
        .reshape(tile_count, tile_rows, feature_width)
    )
    dcandidates = dcandidates + contract("tuc,tud->tcd", counts, daggregate)
    return (loss_sum, dweight, dself, dcandidates)


def per_device(features, boundary, request, tile_slots, neighbors, negatives, layer_weight):
    row_count, feature_width = features.shape
    peer_count = lax.axis_size("group")
    capacity = request.shape[1]
    bound_count = boundary.shape[0]
    block_count = row_count // BLK
    tile_count = tile_slots.shape[0]
    blocks = features.reshape(block_count, BLK, feature_width)
    shared = blocks[boundary].reshape(bound_count * BLK, feature_width)
    published = lax.all_gather(shared, "group", axis=0, tiled=True).reshape(
        peer_count, bound_count, BLK, feature_width
    )
    received = published[jnp.arange(peer_count, dtype=jnp.int32)[:, None], request]
    table_rows = jnp.concatenate(
        [blocks, received.reshape(peer_count * capacity, BLK, feature_width)], axis=0
    )
    slot_list = tile_slots.reshape(-1)
    candidates = table_rows[slot_list].reshape(tile_count, NBT * BLK, feature_width)
    own_rows = features.reshape(tile_count, TILE, feature_width)
    neighbor_ids = neighbors.reshape(tile_count, TILE, DEG)
    negative_ids = negatives.reshape(tile_count, TILE, NNEG)
    loss_sum, dweight, dself, dcandidates = tile_terms(
        own_rows, candidates, neighbor_ids, negative_ids, layer_weight
    )
    table_grad = jnp.zeros((block_count + peer_count * capacity, BLK, feature_width), jnp.float32)
    table_grad = table_grad.at[slot_list].add(dcandidates.reshape(-1, BLK, feature_width))
    own_grad = table_grad[:block_count] + dself.reshape(block_count, BLK, feature_width)
    incoming = table_grad[block_count:]
    sectioned = jnp.zeros((peer_count, bound_count, BLK, feature_width), jnp.float32)
    sectioned = sectioned.at[jnp.arange(peer_count, dtype=jnp.int32)[:, None], request].add(
        incoming.reshape(peer_count, capacity, BLK, feature_width)
    )
    summed_back = lax.psum_scatter(
        sectioned.reshape(peer_count * bound_count * BLK, feature_width),
        "group",
        scatter_dimension=0,
        tiled=True,
    )
    own_grad = own_grad.at[boundary].add(summed_back.reshape(bound_count, BLK, feature_width))
    totals = lax.psum((dweight, loss_sum), ("dom", "group"))
    device_total = lax.axis_size(("dom", "group"))
    return (
        own_grad.reshape(row_count, feature_width),
        totals[0] / row_count,
        totals[1] / (row_count * device_total),
    )


def solution(mesh):
    return jax.shard_map(
        per_device,
        mesh=mesh,
        in_specs=(
            P(("dom", "group"), None),
            P(("dom", "group")),
            P(("dom", "group"), None),
            P(("dom", "group"), None),
            P(("dom", "group"), None),
            P(("dom", "group"), None),
            P(),
        ),
        out_specs=(P(("dom", "group"), None), P(), P()),
        check_vma=False,
    )
```

profile of v0, /device:TPU:0, one launch (start us, length us, event | category | flops | bytes accessed | tf_op | source)
XLA Modules:
  0.0 263.6 jit_solution(1300090860702294701)
XLA Ops:
  7.2 0.0 copy-start
  7.2 0.0 all-gather.2.cloned.1.call-start
  7.2 0.7 compare_select_fusion.2
  7.9 2.7 %gather_fusion = bf16[64,16,256]{2,1,0:T(8,128)(2,1)} fusion(bf16[128,16,256]{2,1,0:T(8,128)(2,1)} %bitcast.70, s32[1024]{0:T(1024)S(1)} %pad_clamp_fusion.1), kind=kCustom, calls=%fused_computation | custom fusion | bytes 1048832 | tf_op jit(solution)/shard_map/gather | solution.py:76
  10.6 0.0 all-gather.2.cloned.1.call-update
  10.7 0.0 all-reduce.2.cloned.1.call-start
  10.7 0.7 fusion.18
  11.4 0.1 reshape.154
  11.5 0.1 reshape.132
  11.6 0.8 copy.22
  12.3 0.1 reshape.110
  12.4 0.9 copy.35
  13.4 4.0 %convert_reduce_fusion = bf16[16,128,128]{2,1,0:T(8,128)(2,1)S(1)} fusion(s32[16,128,10]{1,2,0:T(8,128)S(1)} %copy.24), kind=kLoop, calls=%fused_computation.6 | loop fusion | flops 7602176 | bytes 606208 | tf_op jit(solution)/shard_map/reduce_sum | solution.py:25
  17.5 0.0 copy-start.3
  17.5 18.7 %all-gather.2.cloned.1.call-done = bf16[4096,256]{1,0:T(8,128)(2,1)} async-done(((bf16[1024,256]{1,0:T(8,128)(2,1)}), bf16[4096,256]{1,0:T(8,128)(2,1)}) %all-gather.2.cloned.1.call-update) | async-done | bytes 2097168 | tf_op jit(solution)/shard_map/all_gather | solution.py:77
  36.2 2.6 gather_fusion.1
  38.8 0.0 copy-done.7
  38.8 1.4 pad_maximum_fusion.1
  40.2 2.1 gather_fusion.2
  42.3 0.0 copy-start.8
  42.3 0.0 copy-done.3
  42.3 0.4 multiply_convert_fusion
  42.8 0.0 copy-start.10
  42.8 0.0 copy-done
  42.8 0.8 copy-done.8
  43.5 1.1 multiply_reduce_fusion
  44.7 0.0 copy-done.10
  44.7 0.6 multiply_convert_fusion.1
  45.3 1.0 copy-done.5
  46.3 1.4 select_reduce_fusion.2
  47.7 2.5 copy.25
  50.3 3.9 %select_reduce_fusion.1 = f32[16,128,4]{1,2,0:T(4,128)S(1)} fusion(f32[16,128,128]{2,1,0:T(8,128)} %copy.25, s32[16,128,4]{1,2,0:T(4,128)S(1)} %bitcast.78), kind=kLoop, calls=%fused_computation.9 | loop fusion | flops 3137536 | bytes 1114112 | tf_op jit(solution)/shard_map/reduce_sum | solution.py:41
  54.1 0.7 fusion.26
  54.8 3.8 %select_reduce_fusion = f32[16,128,128]{2,1,0:T(8,128)} fusion(f32[16,128,4]{1,2,0:T(4,128)S(1)} %get-tuple-element.4, s32[16,128,4]{1,2,0:T(4,128)S(1)} %bitcast.79), kind=kLoop, calls=%fused_computation.8 | loop fusion | flops 2883584 | bytes 1114112 | tf_op jit(solution)/shard_map/reduce_sum | solution.py:46
  58.6 2.5 copy.27
  61.1 1.9 fusion.12
  63.0 0.0 copy-done.1
  63.0 0.0 copy-done.6
  63.0 1.7 fusion.13
  64.7 1.0 fusion.1
  65.7 0.0 copy-start.9
  65.8 1.4 fusion.5
  67.2 0.1 copy-done.11
  67.3 1.5 fusion.7
  68.8 2.7 %fusion.27 = f32[2048,512]{1,0:T(8,128)} fusion(bf16[2048,256]{1,0:T(8,128)(2,1)S(1)} %fusion.5, bf16[512,256]{1,0:T(8,128)(2,1)S(1)} %copy-done), kind=kOutput, calls=%fused_computation.70 | convolution fusion | flops 536870912 | bytes 5505024 | tf_op jit(solution)/shard_map/dot_general | solution.py:57
  71.5 0.0 all-reduce.2.cloned.1.call-update
  71.5 0.2 reduce-scatter.2.cloned.1.call-start
  71.8 0.0 copy-start.2
  71.8 2.7 %fusion = (bf16[2048,256]{1,0:T(8,128)(2,1)S(1)}, f32[2048,256]{1,0:T(8,128)S(1)}) fusion(f32[2048,512]{1,0:T(8,128)} %fusion.27), kind=kLoop, calls=%fused_computation.13 | loop fusion | flops 1048576 | bytes 7340032 | tf_op jit(solution)/shard_map/convert_element_type | solution.py:61
  74.5 0.0 copy-done.4
  74.5 0.2 copy-done.2
  74.7 1.8 convolution_add_fusion
  76.5 2.3 broadcast_in_dim.10
  78.8 17.5 %scatter_fusion = f32[224,16,256]{2,1,0:T(8,128)} fusion(f32[224,16,256]{2,1,0:T(8,128)} %broadcast_in_dim.10, s32[128]{0:T(128)S(1)} %fusion.19, f32[128,16,256]{2,1,0:T(8,128)} %bitcast.65), kind=kCustom, calls=%fused_computation.3 | custom fusion | flops 524288 | bytes 6291968 | tf_op jit(solution)/shard_map/scatter-add | solution.py:93
  96.2 2.7 %slice.32 = f32[96,16,256]{2,1,0:T(8,128)} slice(f32[224,16,256]{2,1,0:T(8,128)} %scatter_fusion), slice={[128:224], [0:16], [0:256]} | slice | bytes 3145728 | tf_op jit(solution)/shard_map/slice | solution.py:95
  98.9 2.5 broadcast_in_dim.14
  101.3 14.0 %scatter_fusion.1 = f32[4,64,16,256]{3,2,1,0:T(8,128)} fusion(f32[4,64,16,256]{3,2,1,0:T(8,128)} %broadcast_in_dim.14, s32[96]{0:T(128)S(1)} %reshape.154, f32[96,16,256]{2,1,0:T(8,128)} %slice.32), kind=kCustom, calls=%fused_computation.4 | custom fusion | flops 393216 | bytes 4719360 | tf_op jit(solution)/shard_map/scatter-add | solution.py:97
  115.3 0.0 reduce-scatter.2.cloned.1.call-update
  116.0 39.3 %psum.15 = f32[]{:T(128)} all-reduce(f32[]{:T(128)S(6)} %div.58), channel_id=1, replica_groups=mesh['dom'=8,'group'=4] {'dom','group'}, use_global_device_ids=true, to_apply=%region_13.14 | all-reduce | flops 1 | bytes 8 | tf_op jit(solution)/shard_map/psum | solution.py:107
  156.0 3.4 %slice_add_fusion = f32[128,16,256]{2,1,0:T(8,128)} fusion(f32[128,16,256]{2,1,0:T(8,128)S(1)} %bitcast.64, f32[224,16,256]{2,1,0:T(8,128)} %scatter_fusion), kind=kLoop, calls=%fused_computation.11 | loop fusion | flops 524288 | bytes 6291456 | tf_op jit(solution)/shard_map/add | solution.py:94
  159.4 41.4 %all-reduce.2.cloned.1.call-done = f32[512,256]{1,0:T(8,128)} async-done(((f32[512,256]{1,0:T(8,128)}), f32[512,256]{1,0:T(8,128)}) %all-reduce.2.cloned.1.call-update) | async-done | bytes 524304 | tf_op jit(solution)/shard_map/psum | solution.py:107
  200.8 1.9 broadcast_multiply_fusion
  202.7 44.3 %reduce-scatter.2.cloned.1.call-done = f32[1024,256]{1,0:T(8,128)} async-done(((f32[4096,256]{1,0:T(8,128)}), f32[1024,256]{1,0:T(8,128)}) %reduce-scatter.2.cloned.1.call-update) | async-done | bytes 1048592 | tf_op jit(solution)/shard_map/reduce_scatter | solution.py:100
  247.0 9.0 %scatter_fusion.2 = f32[128,16,256]{2,1,0:T(8,128)} fusion(f32[128,16,256]{2,1,0:T(8,128)} %slice_add_fusion, s32[64]{0:T(128)S(1)} %compare_select_fusion.2, f32[64,16,256]{2,1,0:T(8,128)} %bitcast.75), kind=kCustom, calls=%fused_computation.5 | custom fusion | flops 262144 | bytes 3145984 | tf_op jit(solution)/shard_map/scatter-add | solution.py:106
  (17 shorter events, 0.1 us)
Async XLA Ops:
  7.2 35.6 %copy-start = (bf16[512,256]{1,0:T(8,128)(2,1)S(1)}, bf16[512,256]{1,0:T(8,128)(2,1)}, u32[]{:S(2)}) copy-start(bf16[512,256]{1,0:T(8,128)(2,1)} %param.13) | copy-start | bytes 786436
  7.2 29.0 %all-gather.2.cloned.1.call-start = ((), (), s32[]{:S(2)}) async-start(), calls=%async_computation.1 | async-start | bytes 2621440 | tf_op jit(solution)/shard_map/all_gather | solution.py:77
  7.9 30.8 %copy-start.7 = (bf16[2048,256]{1,0:T(8,128)(2,1)S(1)}, bf16[2048,256]{1,0:T(8,128)(2,1)}, u32[]{:S(2)}) copy-start(bf16[2048,256]{1,0:T(8,128)(2,1)} %param.7) | copy-start | bytes 3145732
  10.7 190.2 %all-reduce.2.cloned.1.call-start = ((), (), s32[]{:S(2)}) async-start(), calls=%async_computation.3 | async-start | bytes 1048576 | tf_op jit(solution)/shard_map/psum | solution.py:107
  17.5 24.9 %copy-start.3 = (bf16[16,128,128]{2,1,0:T(8,128)(2,1)}, bf16[16,128,128]{2,1,0:T(8,128)(2,1)S(1)}, u32[]{:S(2)}) copy-start(bf16[16,128,128]{2,1,0:T(8,128)(2,1)S(1)} %convert_reduce_fusion) | copy-start | bytes 1572868
  42.3 1.2 copy-start.8
  42.8 1.9 copy-start.10
  45.3 1.0 copy-start.5
  46.3 4.0 %copy-start.12 = (s32[2048,4]{0,1:T(4,128)S(1)}, s32[2048,4]{0,1:T(4,128)}, u32[]{:S(2)}) copy-start(s32[2048,4]{0,1:T(4,128)} %param.12) | copy-start | bytes 98308
  61.1 1.9 copy-start.1
  61.1 1.9 copy-start.6
  65.7 1.5 copy-start.9
  65.8 1.5 copy-start.11
  71.5 3.0 %copy-start.4 = (bf16[16,128,128]{2,1,0:T(8,128)(2,1)S(1)}, bf16[16,128,128]{2,1,0:T(8,128)(2,1)}, u32[]{:S(2)}) copy-start(bf16[16,128,128]{2,1,0:T(8,128)(2,1)} %copy-done.3) | copy-start | bytes 1572868
  71.5 175.4 %reduce-scatter.2.cloned.1.call-start = ((), (), s32[]{:S(2)}) async-start(), calls=%async_computation.2 | async-start | bytes 5242880 | tf_op jit(solution)/shard_map/reduce_scatter | solution.py:100
  71.8 2.9 %copy-start.2 = (f32[16,128,256]{2,1,0:T(8,128)S(1)}, f32[16,128,256]{2,1,0:T(8,128)}, u32[]{:S(2)}) copy-start(f32[16,128,256]{2,1,0:T(8,128)} %fusion.13) | copy-start | bytes 6291460
Sparse Core Ops, SparseCore 0:
  10.8 25.3 all-gather.1
  71.6 129.1 all-reduce.1
  203.3 43.5 reduce-scatter.1
where the time goes:
time: 265 us; the launch traced here: 264 us
  waiting for transfers between devices  104 us (39%)
  other arithmetic  66.5 us (25%)
  blocking collectives  39.3 us (15%)
  local copies, waits for them, and re-layouts  24 us (9%)
  between operations  16.5 us (6%)
  matrix products  12.6 us (5%)
    reduce_scatter x1, waiting for transfers between devices, per_device(): lax.psum_scatter(sectioned.reshape(peer_count * bound_count * BLK, featur...  44.3 us
    psum x1, waiting for transfers between devices, per_device(): totals = lax.psum((dweight, loss_sum), ('dom', 'group'))  41.4 us
    psum x1, blocking collectives, per_device(): totals = lax.psum((dweight, loss_sum), ('dom', 'group'))  39.3 us
    all_gather x1, waiting for transfers between devices, per_device(): lax.all_gather(shared, 'group', axis=0, tiled=True)  18.7 us
    scatter-add x1, other arithmetic, per_device(): table_grad.at[slot_list].add(dcandidates.reshape(-1, BLK, feature_width))  17.5 us
    scatter-add x1, other arithmetic, per_device(): sectioned.at[jnp.arange(peer_count, dtype=jnp.int32)[:, None], request]  14 us
    scatter-add x1, other arithmetic, per_device(): own_grad.at[boundary]  9 us
    dot_general x5, matrix products, contract(): return jnp.einsum(form, left, right, preferred_element_type=jnp.float32)  7.26 us
  transfers between devices with their start and end apart: 3, of which 3 were waited for; matrix products, arithmetic and copies ran while one was open for 21% of the time, Pallas kernels for 0%

commit v1 on v0

--- a/solution.py
+++ b/solution.py
@@ -10,6 +10,24 @@
 NNEG = 4
 margin = 0.5
 epsilon = 1e-06
+
+
+def spans_report(view):
+    row_axis = "group"
+    step_out = lax.axis_size(row_axis)
+    y1 = lax.axis_index(row_axis)
+    local_now, built, outcome_arr = (step_out, y1, view.shape[0])
+    steps_seen = [(dev_j, (dev_j + 1) % local_now) for dev_j in range(local_now)]
+    p_next = jnp.zeros((*view.shape[:0], local_now * outcome_arr, *view.shape[1:]), view.dtype)
+    placed = view
+    b = 0
+    while b < local_now:
+        w1 = (built - b) % local_now
+        p_next = lax.dynamic_update_slice_in_dim(p_next, placed, w1 * outcome_arr, axis=0)
+        if b < local_now - 1:
+            placed = lax.ppermute(placed, row_axis, steps_seen)
+        b += 1
+    return p_next
 
 
 def contract(form, left, right):
@@ -74,9 +92,7 @@
     tile_count = tile_slots.shape[0]
     blocks = features.reshape(block_count, BLK, feature_width)
     shared = blocks[boundary].reshape(bound_count * BLK, feature_width)
-    published = lax.all_gather(shared, "group", axis=0, tiled=True).reshape(
-        peer_count, bound_count, BLK, feature_width
-    )
+    published = spans_report(shared).reshape(peer_count, bound_count, BLK, feature_width)
     received = published[jnp.arange(peer_count, dtype=jnp.int32)[:, None], request]
     table_rows = jnp.concatenate(
         [blocks, received.reshape(peer_count * capacity, BLK, feature_width)], axis=0

time: 265 us -> 242 us (0.913)
  waiting for transfers between devices: 104 us -> 72.8 us
    reduce_scatter x1, waiting for transfers between devices: 44.3 us -> 0.01 us  [per_device(): lax.psum_scatter(sectioned.reshape(peer_count * bound_count * BLK, featur...]
    all_gather x1 -> x0, waiting for transfers between devices: 18.7 us -> none  [per_device(): lax.all_gather(shared, 'group', axis=0, tiled=True)]
    ppermute x0 -> x3, waiting for transfers between devices: none -> 17 us  [spans_report(): placed = lax.ppermute(placed, row_axis, steps_seen)]
    psum x1, waiting for transfers between devices: 41.4 us -> 55.8 us  [per_device(): totals = lax.psum((dweight, loss_sum), ('dom', 'group'))]
    dynamic_update_slice x0 -> x4, local copies, waits for them, and re-layouts: none -> 3.47 us  [spans_report(): lax.dynamic_update_slice_in_dim(p_next, placed, w1 * outcome_arr, axis=0)]
  transfers between devices with their start and end apart: 3 -> 5, of which waited for: 3 -> 4; matrix products, arithmetic and copies ran while one was open for 21% -> 24% of each run, Pallas kernels for 0% -> 0%
where the time goes in v1:
time: 242 us; the launch traced here: 240 us
  waiting for transfers between devices  72.8 us (30%)
  other arithmetic  67.9 us (28%)
  blocking collectives  41.8 us (17%)
  local copies, waits for them, and re-layouts  26.2 us (11%)
  between operations  18.3 us (8%)
  matrix products  12.6 us (5%)
    psum x1, waiting for transfers between devices, per_device(): totals = lax.psum((dweight, loss_sum), ('dom', 'group'))  55.8 us
    psum x1, blocking collectives, per_device(): totals = lax.psum((dweight, loss_sum), ('dom', 'group'))  41.8 us
    scatter-add x1, other arithmetic, per_device(): table_grad.at[slot_list].add(dcandidates.reshape(-1, BLK, feature_width))  17.5 us
    ppermute x3, waiting for transfers between devices, spans_report(): placed = lax.ppermute(placed, row_axis, steps_seen)  17 us
    scatter-add x1, other arithmetic, per_device(): sectioned.at[jnp.arange(peer_count, dtype=jnp.int32)[:, None], request]  14 us
    scatter-add x1, other arithmetic, per_device(): own_grad.at[boundary]  9 us
    dot_general x5, matrix products, contract(): return jnp.einsum(form, left, right, preferred_element_type=jnp.float32)  7.26 us
  transfers between devices with their start and end apart: 5, of which 4 were waited for; matrix products, arithmetic and copies ran while one was open for 24% of the time, Pallas kernels for 0%

profile of v1, /device:TPU:0, one launch (start us, length us, event | category | flops | bytes accessed | tf_op | source)
XLA Modules:
  0.0 240.4 jit_solution(17279074850848594796)
XLA Ops:
  8.0 0.0 copy-start
  8.0 0.0 all-reduce.2.cloned.1.call-start
  8.1 0.7 compare_select_fusion.2
  8.8 1.8 gather_fusion
  10.6 0.5 collective-permute-start
  11.1 0.8 copy.22
  11.9 0.1 reshape.110
  12.0 0.9 copy.35
  12.9 0.7 fusion.18
  13.6 6.3 %collective-permute-done = bf16[1024,256]{1,0:T(8,128)(2,1)S(1)} collective-permute-done((bf16[1024,256]{1,0:T(8,128)(2,1)S(1)}, bf16[1024,256]{1,0:T(8,128)(2,1)S(1)}, u32[]{:S(2)}, u32[]{:S(2)}) %collective-permute-start) | collective-permute-done | bytes 524320 | tf_op jit(solution)/shard_map/ppermute | solution.py:28
  19.9 0.0 collective-permute-start.1
  19.9 0.1 broadcast_in_dim.13
  20.2 8.5 %collective-permute-done.1 = bf16[1024,256]{1,0:T(8,128)(2,1)} collective-permute-done((bf16[1024,256]{1,0:T(8,128)(2,1)S(1)}, bf16[1024,256]{1,0:T(8,128)(2,1)}, u32[]{:S(2)}, u32[]{:S(2)}) %collective-permute-start.1) | collective-permute-done | bytes 524320 | tf_op jit(solution)/shard_map/ppermute | solution.py:28
  28.7 0.0 collective-permute-start.2
  28.7 0.0 copy-done.11
  28.8 0.1 reshape.154
  28.9 0.1 reshape.132
  28.9 4.0 %convert_reduce_fusion = bf16[16,128,128]{2,1,0:T(8,128)(2,1)S(1)} fusion(s32[16,128,10]{1,2,0:T(8,128)S(1)} %copy.24), kind=kLoop, calls=%fused_computation.6 | loop fusion | flops 7602176 | bytes 606208 | tf_op jit(solution)/shard_map/reduce_sum | solution.py:43
  33.0 1.3 constant_dynamic-update-slice_fusion.2
  34.3 1.1 constant_dynamic-update-slice_fusion.1
  35.3 2.2 collective-permute-done.2
  37.6 1.1 constant_dynamic-update-slice_fusion
  38.7 2.0 gather_fusion.1
  40.7 2.9 %pad_maximum_fusion.1 = bf16[224,16,256]{2,1,0:T(8,128)(2,1)} fusion(bf16[96,16,256]{2,1,0:T(8,128)(2,1)} %gather_fusion.1, bf16[128,16,256]{2,1,0:T(8,128)(2,1)} %bitcast.72), kind=kLoop, calls=%fused_computation.27 | loop fusion | flops 917504 | bytes 3670016 | tf_op jit(solution)/shard_map/concatenate | solution.py:97
  43.5 2.1 gather_fusion.2
  45.7 0.0 copy-start.7
  45.7 0.4 multiply_convert_fusion
  46.2 0.8 copy-done.7
  46.9 1.1 multiply_reduce_fusion
  48.1 0.6 multiply_convert_fusion.1
  48.6 1.0 copy-done.5
  49.7 1.4 select_reduce_fusion.2
  51.1 2.5 %copy.25 = f32[16,128,128]{2,1,0:T(8,128)} copy(f32[16,128,128]{1,2,0:T(8,128)} %get-tuple-element.13) | data formatting | bytes 2097152 | tf_op jit(solution)/shard_map/mul | solution.py:55
  53.6 3.9 %select_reduce_fusion.1 = f32[16,128,4]{1,2,0:T(4,128)S(1)} fusion(f32[16,128,128]{2,1,0:T(8,128)} %copy.25, s32[16,128,4]{1,2,0:T(4,128)S(1)} %bitcast.79), kind=kLoop, calls=%fused_computation.9 | loop fusion | flops 3137536 | bytes 1114112 | tf_op jit(solution)/shard_map/reduce_sum | solution.py:59
  57.5 0.7 fusion.26
  58.2 3.8 %select_reduce_fusion = f32[16,128,128]{2,1,0:T(8,128)} fusion(f32[16,128,4]{1,2,0:T(4,128)S(1)} %get-tuple-element.4, s32[16,128,4]{1,2,0:T(4,128)S(1)} %bitcast.80), kind=kLoop, calls=%fused_computation.8 | loop fusion | flops 2883584 | bytes 1114112 | tf_op jit(solution)/shard_map/reduce_sum | solution.py:64
  61.9 2.5 %copy.27 = f32[16,128,128]{1,2,0:T(8,128)} copy(f32[16,128,128]{2,1,0:T(8,128)} %select_reduce_fusion) | data formatting | bytes 2097152 | tf_op jit(solution)/shard_map/reduce_sum | solution.py:64
  64.5 1.9 fusion.12
  66.3 0.0 copy-done.1
  66.4 0.0 copy-done.6
  66.4 1.7 fusion.13
  68.1 1.0 fusion.1
  69.1 0.0 copy-start.8
  69.1 1.4 fusion.5
  70.6 0.1 copy-done.10
  70.7 1.5 fusion.7
  72.2 2.7 %fusion.27 = f32[2048,512]{1,0:T(8,128)} fusion(bf16[2048,256]{1,0:T(8,128)(2,1)S(1)} %fusion.5, bf16[512,256]{1,0:T(8,128)(2,1)S(1)} %copy-done), kind=kOutput, calls=%fused_computation.74 | convolution fusion | flops 536870912 | bytes 5505024 | tf_op jit(solution)/shard_map/dot_general | solution.py:75
  74.9 0.0 all-reduce.2.cloned.1.call-update
  74.9 0.2 reduce-scatter.2.cloned.1.call-start
  75.1 0.0 copy-start.2
  75.2 2.7 %fusion = (bf16[2048,256]{1,0:T(8,128)(2,1)S(1)}, f32[2048,256]{1,0:T(8,128)S(1)}) fusion(f32[2048,512]{1,0:T(8,128)} %fusion.27), kind=kLoop, calls=%fused_computation.13 | loop fusion | flops 1048576 | bytes 7340032 | tf_op jit(solution)/shard_map/convert_element_type | solution.py:79
  77.9 0.2 copy-done.2
  78.0 1.8 convolution_add_fusion
  79.8 2.3 broadcast_in_dim.12
  82.1 17.5 %scatter_fusion = f32[224,16,256]{2,1,0:T(8,128)} fusion(f32[224,16,256]{2,1,0:T(8,128)} %broadcast_in_dim.12, s32[128]{0:T(128)S(1)} %fusion.19, f32[128,16,256]{2,1,0:T(8,128)} %bitcast.65), kind=kCustom, calls=%fused_computation.3 | custom fusion | flops 524288 | bytes 6291968 | tf_op jit(solution)/shard_map/scatter-add | solution.py:109
  99.6 2.7 %slice.32 = f32[96,16,256]{2,1,0:T(8,128)} slice(f32[224,16,256]{2,1,0:T(8,128)} %scatter_fusion), slice={[128:224], [0:16], [0:256]} | slice | bytes 3145728 | tf_op jit(solution)/shard_map/slice | solution.py:111
  102.3 2.5 %broadcast_in_dim.17 = f32[4,64,16,256]{3,2,1,0:T(8,128)} broadcast(f32[]{:T(128)} %constant.73.clone.1), dimensions={} | broadcast | bytes 4194308 | tf_op jit(solution)/shard_map/broadcast_in_dim | solution.py:112
  104.7 14.0 %scatter_fusion.1 = f32[4,64,16,256]{3,2,1,0:T(8,128)} fusion(f32[4,64,16,256]{3,2,1,0:T(8,128)} %broadcast_in_dim.17, s32[96]{0:T(128)S(1)} %reshape.154, f32[96,16,256]{2,1,0:T(8,128)} %slice.32), kind=kCustom, calls=%fused_computation.4 | custom fusion | flops 393216 | bytes 4719360 | tf_op jit(solution)/shard_map/scatter-add | solution.py:113
  118.7 0.0 reduce-scatter.2.cloned.1.call-update
  119.4 41.8 %psum.15 = f32[]{:T(128)} all-reduce(f32[]{:T(128)S(6)} %div.58), channel_id=1, replica_groups=mesh['dom'=8,'group'=4] {'dom','group'}, use_global_device_ids=true, to_apply=%region_13.14 | all-reduce | flops 1 | bytes 8 | tf_op jit(solution)/shard_map/psum | solution.py:123
  161.8 3.4 %slice_add_fusion = f32[128,16,256]{2,1,0:T(8,128)} fusion(f32[128,16,256]{2,1,0:T(8,128)S(1)} %bitcast.64, f32[224,16,256]{2,1,0:T(8,128)} %scatter_fusion), kind=kLoop, calls=%fused_computation.11 | loop fusion | flops 524288 | bytes 6291456 | tf_op jit(solution)/shard_map/add | solution.py:110
  165.2 55.8 %all-reduce.2.cloned.1.call-done = f32[512,256]{1,0:T(8,128)} async-done(((f32[512,256]{1,0:T(8,128)}), f32[512,256]{1,0:T(8,128)}) %all-reduce.2.cloned.1.call-update) | async-done | bytes 524304 | tf_op jit(solution)/shard_map/psum | solution.py:123
  221.0 1.9 broadcast_multiply_fusion
  222.9 9.0 %scatter_fusion.2 = f32[128,16,256]{2,1,0:T(8,128)} fusion(f32[128,16,256]{2,1,0:T(8,128)} %slice_add_fusion, s32[64]{0:T(128)S(1)} %compare_select_fusion.2, f32[64,16,256]{2,1,0:T(8,128)} %bitcast.77), kind=kCustom, calls=%fused_computation.5 | custom fusion | flops 262144 | bytes 3145984 | tf_op jit(solution)/shard_map/scatter-add | solution.py:122
  (25 shorter events, 0.1 us)
Async XLA Ops:
  8.0 38.2 %copy-start = (bf16[512,256]{1,0:T(8,128)(2,1)S(1)}, bf16[512,256]{1,0:T(8,128)(2,1)}, u32[]{:S(2)}) copy-start(bf16[512,256]{1,0:T(8,128)(2,1)} %param.13) | copy-start | bytes 786436
  8.0 213.0 %all-reduce.2.cloned.1.call-start = ((), (), s32[]{:S(2)}) async-start(), calls=%async_computation.2 | async-start | bytes 1048576 | tf_op jit(solution)/shard_map/psum | solution.py:123
  10.6 9.4 %collective-permute-start = (bf16[1024,256]{1,0:T(8,128)(2,1)S(1)}, bf16[1024,256]{1,0:T(8,128)(2,1)S(1)}, u32[]{:S(2)}, u32[]{:S(2)}) collective-permute-start(bf16[1024,256]{1,0:T(8,128)(2,1)S(1)} %bitcast.73), channel_id=1, source_target_pairs={{0,1},{1,2},{2,3},{3,0},{4,5},{5,6},{6,7},{7,4},{8,9},{9,10},{10,1... | collective-permute-start | bytes 1572872 | tf_op jit(solution)/shard_map/ppermute | solution.py:28
  19.9 8.8 %copy-start.11 = (bf16[1024,256]{1,0:T(8,128)(2,1)}, bf16[1024,256]{1,0:T(8,128)(2,1)S(1)}, u32[]{:S(2)}) copy-start(bf16[1024,256]{1,0:T(8,128)(2,1)S(1)} %collective-permute-done) | copy-start | bytes 1572868
  19.9 8.7 %collective-permute-start.1 = (bf16[1024,256]{1,0:T(8,128)(2,1)S(1)}, bf16[1024,256]{1,0:T(8,128)(2,1)}, u32[]{:S(2)}, u32[]{:S(2)}) collective-permute-start(bf16[1024,256]{1,0:T(8,128)(2,1)S(1)} %collective-permute-done), channel_id=1, source_target_pairs={{0,1},{1,2},{2,3},{3,0},{4,5},{5,6},{6,7},{7,4},{8,9},{9,10},{10,1... | collective-permute-start | bytes 1572872 | tf_op jit(solution)/shard_map/ppermute | solution.py:28
  28.7 8.9 %collective-permute-start.2 = (bf16[1024,256]{1,0:T(8,128)(2,1)}, bf16[1024,256]{1,0:T(8,128)(2,1)}, u32[]{:S(2)}, u32[]{:S(2)}) collective-permute-start(bf16[1024,256]{1,0:T(8,128)(2,1)} %collective-permute-done.1), channel_id=1, source_target_pairs={{0,1},{1,2},{2,3},{3,0},{4,5},{5,6},{6,7},{7,4},{8,9},{9,10},{10,1... | collective-permute-start | bytes 1572872 | tf_op jit(solution)/shard_map/ppermute | solution.py:28
  33.0 12.7 %copy-start.3 = (bf16[16,128,128]{2,1,0:T(8,128)(2,1)}, bf16[16,128,128]{2,1,0:T(8,128)(2,1)S(1)}, u32[]{:S(2)}) copy-start(bf16[16,128,128]{2,1,0:T(8,128)(2,1)S(1)} %convert_reduce_fusion) | copy-start | bytes 1572868
  45.7 1.2 copy-start.7
  46.1 1.9 copy-start.9
  48.6 1.0 copy-start.5
  49.7 4.0 %copy-start.12 = (s32[2048,4]{0,1:T(4,128)S(1)}, s32[2048,4]{0,1:T(4,128)}, u32[]{:S(2)}) copy-start(s32[2048,4]{0,1:T(4,128)} %param.12) | copy-start | bytes 98308
  64.5 1.9 copy-start.1
  64.5 1.9 copy-start.6
  69.1 1.5 copy-start.8
  69.1 1.5 copy-start.10
  74.9 3.0 %copy-start.4 = (bf16[16,128,128]{2,1,0:T(8,128)(2,1)S(1)}, bf16[16,128,128]{2,1,0:T(8,128)(2,1)}, u32[]{:S(2)}) copy-start(bf16[16,128,128]{2,1,0:T(8,128)(2,1)} %copy-done.3) | copy-start | bytes 1572868
  74.9 147.9 %reduce-scatter.2.cloned.1.call-start = ((), (), s32[]{:S(2)}) async-start(), calls=%async_computation.1 | async-start | bytes 5242880 | tf_op jit(solution)/shard_map/reduce_scatter | solution.py:116
  75.1 2.9 %copy-start.2 = (f32[16,128,256]{2,1,0:T(8,128)S(1)}, f32[16,128,256]{2,1,0:T(8,128)}, u32[]{:S(2)}) copy-start(f32[16,128,256]{2,1,0:T(8,128)} %fusion.13) | copy-start | bytes 6291460
Sparse Core Ops, SparseCore 0:
  75.0 145.9 all-reduce.1
Sparse Core Ops, SparseCore 1:
  118.8 47.2 reduce-scatter.1
